TPU v7x, 32 devices: a whole 2x2x4 slice. The times are simulated.
32 devices in a mesh: clips: 2 (over y), seq: 4 (over z), tp: 2 (over x), dp: 2 (over core).
Axes of the slice: x: 2, y: 2, z: 4, core: 2. Of those that a mesh axis runs over, the one named last changes fastest.
Arguments:
- video_query: bfloat16 [4, 512, 4096], P(('clips', 'dp'), 'seq', 'tp'), parts along dimension 0, may hold values from -384 to 384
- video_key: bfloat16 [4, 512, 4096], P(('clips', 'dp'), 'seq', 'tp'), parts along dimension 0, may hold values from -384 to 384
- video_value: bfloat16 [4, 512, 4096], P(('clips', 'dp'), 'seq', 'tp'), parts along dimension 0, may hold values from -6 to 6
- cross_query: bfloat16 [4, 512, 2048], P(('clips', 'dp'), 'seq', 'tp'), parts along dimension 0, may hold values from -384 to 384
- audio_key: bfloat16 [4, 32, 2048], P(('clips', 'dp'), 'seq', 'tp'), parts along dimension 0, may hold values from -384 to 384
- audio_value: bfloat16 [4, 32, 2048], P(('clips', 'dp'), 'seq', 'tp'), parts along dimension 0, may hold values from -6 to 6
- audio_query: bfloat16 [4, 32, 2048], P(('clips', 'dp'), 'seq', 'tp'), parts along dimension 0, may hold values from -384 to 384
- cross_key: bfloat16 [4, 512, 2048], P(('clips', 'dp'), 'seq', 'tp'), parts along dimension 0, may hold values from -384 to 384
- cross_value: bfloat16 [4, 512, 2048], P(('clips', 'dp'), 'seq', 'tp'), parts along dimension 0, may hold values from -6 to 6
- audio_input: bfloat16 [4, 32, 2048], P(('clips', 'dp'), 'seq'), parts along dimension 0, may hold values from -0.29882812 to 0.29882812
- norm_gain: float32 [2048], replicated, may hold values from 0.1 to 1.9
- up_weight: bfloat16 [2048, 8192], P('tp', 'seq'), may hold values from -0.125 to 0.125
- down_weight: bfloat16 [8192, 2048], P('seq', 'tp'), may hold values from -0.0625 to 0.0625
Outputs:
- video_mixed: bfloat16 [4, 512, 4096], P(('clips', 'dp'), 'seq', 'tp'), parts along dimension 0
- video_heard: bfloat16 [4, 512, 2048], P(('clips', 'dp'), 'seq', 'tp'), parts along dimension 0
- audio_seen: bfloat16 [4, 32, 2048], P(('clips', 'dp'), 'seq', 'tp'), parts along dimension 0
- audio_mlp: bfloat16 [4, 32, 2048], P(('clips', 'dp'), 'seq', 'tp'), parts along dimension 0
There are 2 independent parts, one for each index of `clips`. A program takes and returns all parts, laid end to end along the dimension named above; an argument that names none is the same for every part. Nothing has to cross between parts.
All inputs are finite; a program needn't handle non-finite values.
Results may differ from a plain program's by a relative error of at most 0.013.
Values may be sent and summed in bfloat16 or wider, within the bound.
A program may use at most 64 MiB of HBM per device.

v0:
```python
import math
import jax
import jax.numpy as jnp
from jax import lax
from jax.sharding import PartitionSpec as P

VHEAD = 128
CHEAD = 64


def attend_rows(queries, keys_in, values_in, head_count):
    head_size = queries.shape[1] // head_count
    query_heads = queries.reshape(queries.shape[0], head_count, head_size)
    key_heads = keys_in.reshape(keys_in.shape[0], head_count, head_size)
    value_heads = values_in.reshape(values_in.shape[0], head_count, head_size)
    scores = jnp.einsum(
        "qhd,khd->qhk", query_heads, key_heads, preferred_element_type=jnp.float32
    ) / math.sqrt(head_size)
    peak_value = jnp.max(scores, axis=2, keepdims=True)
    weights = jnp.exp(scores - peak_value)
    totals = jnp.sum(weights, axis=2)
    weighted = jnp.einsum(
        "qhk,khd->qhd",
        weights.astype(jnp.bfloat16),
        value_heads,
        preferred_element_type=jnp.float32,
    )
    result = weighted / totals[:, :, None]
    return result.reshape(queries.shape[0], head_count * head_size).astype(jnp.bfloat16)


def attend(queries, keys_in, values_in, head_count):
    row_total = queries.shape[0]
    block_rows = 512 if row_total % 512 == 0 else row_total
    pieces = queries.reshape(row_total // block_rows, block_rows, queries.shape[1])
    result = lax.map(
        lambda row_piece: attend_rows(row_piece, keys_in, values_in, head_count), pieces
    )
    return result.reshape(row_total, queries.shape[1])


def video_self(queries, keys_in, values_in):
    seq_count = lax.axis_size("seq")
    local_heads = queries.shape[1] // VHEAD
    dest_heads = max(local_heads // seq_count, 1)
    blocks = seq_count * dest_heads // local_heads
    groups = local_heads // dest_heads
    group_width = dest_heads * VHEAD
    token_count = queries.shape[0]
    block_tokens = token_count // blocks

    def spread(tensor):
        shaped = tensor.reshape(token_count, groups, group_width).transpose(1, 0, 2)
        shaped = jnp.broadcast_to(shaped[:, None], (groups, blocks, token_count, group_width))
        return shaped.reshape(seq_count, token_count, group_width)

    shaped = queries.reshape(blocks, block_tokens, groups, group_width).transpose(2, 0, 1, 3)
    own_queries = lax.all_to_all(
        shaped.reshape(seq_count, block_tokens, group_width),
        "seq",
        split_axis=0,
        concat_axis=0,
        tiled=True,
    )
    keys_all = lax.all_to_all(spread(keys_in), "seq", split_axis=0, concat_axis=0, tiled=True)
    values_all = lax.all_to_all(spread(values_in), "seq", split_axis=0, concat_axis=0, tiled=True)
    keys_all = keys_all.reshape(-1, group_width)
    values_all = values_all.reshape(-1, group_width)
    own_queries = own_queries.reshape(-1, group_width)
    attended = attend(own_queries, keys_all, values_all, dest_heads)
    returned = lax.all_to_all(
        attended.reshape(seq_count, block_tokens, group_width),
        "seq",
        split_axis=0,
        concat_axis=0,
        tiled=True,
    )
    returned = returned.reshape(groups, blocks, block_tokens, group_width).transpose(1, 2, 0, 3)
    return returned.reshape(token_count, groups * group_width)


def audio_listen(queries, keys_in, values_in, head_count):
    head_size = queries.shape[1] // head_count
    query_heads = queries.reshape(queries.shape[0], head_count, head_size)
    key_heads = keys_in.reshape(keys_in.shape[0], head_count, head_size)
    value_heads = values_in.reshape(values_in.shape[0], head_count, head_size)
    scores = jnp.einsum(
        "qhd,khd->qhk", query_heads, key_heads, preferred_element_type=jnp.float32
    ) / math.sqrt(head_size)
    local_peak = jnp.max(scores, axis=2)
    peak_value = lax.pmax(local_peak, "seq")
    weights = jnp.exp(scores - peak_value[:, :, None])
    totals = jnp.sum(weights, axis=2)
    weighted = jnp.einsum(
        "qhk,khd->qhd",
        weights.astype(jnp.bfloat16),
        value_heads,
        preferred_element_type=jnp.float32,
    )
    totals, weighted = (totals, weighted.reshape(queries.shape[0], head_count * head_size))
    totals, weighted = (
        lax.psum_scatter(totals, "seq", scatter_dimension=0, tiled=True),
        lax.psum_scatter(weighted, "seq", scatter_dimension=0, tiled=True),
    )
    return (weighted / jnp.repeat(totals, head_size, axis=1)).astype(jnp.bfloat16)


def audio_block(audio_rows, audio_seen, norm_gain, up_weight, down_weight):
    features = lax.all_gather(audio_seen, "tp", axis=1, tiled=True)
    residual = audio_rows.astype(jnp.float32) + features.astype(jnp.float32)
    scale_factor = lax.rsqrt(jnp.mean(residual * residual, axis=1, keepdims=True) + 1e-06)
    normed = (residual * scale_factor * norm_gain).astype(jnp.bfloat16)
    slice_width = up_weight.shape[0]
    own_features = lax.dynamic_slice_in_dim(
        normed, lax.axis_index("tp") * slice_width, slice_width, 1
    )
    partial_sum = jnp.dot(
        lax.all_gather(own_features, "seq", axis=0, tiled=True),
        up_weight,
        preferred_element_type=jnp.float32,
    )
    hidden = jax.nn.gelu(lax.psum(partial_sum, "tp")).astype(jnp.bfloat16)
    return lax.psum_scatter(
        jnp.dot(hidden, down_weight, preferred_element_type=jnp.float32),
        "seq",
        scatter_dimension=0,
        tiled=True,
    ).astype(jnp.bfloat16)


def body(
    video_query,
    video_key,
    video_value,
    cross_query,
    audio_key,
    audio_value,
    audio_query,
    cross_key,
    cross_value,
    audio_input,
    norm_gain,
    up_weight,
    down_weight,
):
    mixed_list, heard_list, seen_list, output_list = ([], [], [], [])
    cross_heads = cross_query.shape[2] // CHEAD
    mixed_list.append(video_self(video_query[0], video_key[0], video_value[0]))
    gathered_query = lax.all_gather(audio_query[0], "seq", axis=0, tiled=True)
    gathered_key = lax.all_gather(audio_key[0], "seq", axis=0, tiled=True)
    gathered_value = lax.all_gather(audio_value[0], "seq", axis=0, tiled=True)
    heard_list.append(attend(cross_query[0], gathered_key, gathered_value, cross_heads))
    audio_seen = audio_listen(gathered_query, cross_key[0], cross_value[0], cross_heads)
    seen_list.append(audio_seen)
    output_list.append(audio_block(audio_input[0], audio_seen, norm_gain, up_weight, down_weight))
    return (
        jnp.stack(mixed_list),
        jnp.stack(heard_list),
        jnp.stack(seen_list),
        jnp.stack(output_list),
    )


def solution(mesh):
    placed = (
        P(("clips", "dp"), "seq", "tp"),
        P(("clips", "dp"), "seq", "tp"),
        P(("clips", "dp"), "seq", "tp"),
        P(("clips", "dp"), "seq", "tp"),
        P(("clips", "dp"), "seq", "tp"),
        P(("clips", "dp"), "seq", "tp"),
        P(("clips", "dp"), "seq", "tp"),
        P(("clips", "dp"), "seq", "tp"),
        P(("clips", "dp"), "seq", "tp"),
        P(("clips", "dp"), "seq", None),
        P(),
        P("tp", "seq"),
        P("seq", "tp"),
    )
    return jax.shard_map(
        body,
        mesh=mesh,
        in_specs=placed,
        out_specs=(
            P(("clips", "dp"), "seq", "tp"),
            P(("clips", "dp"), "seq", "tp"),
            P(("clips", "dp"), "seq", "tp"),
            P(("clips", "dp"), "seq", "tp"),
        ),
        check_vma=False,
    )
```

profile of v0, /device:TPU:0, one launch (start us, length us, event | category | flops | bytes accessed | tf_op | source)
XLA Modules:
  0.0 171.0 jit_solution(16451558797304456168)
XLA Ops:
  7.2 2.0 %copy.100 = bf16[1,16,4,8,512]{4,3,1,2,0:T(8,128)(2,1)} copy(bf16[1,16,4,8,512]{4,3,2,1,0:T(8,128)(2,1)} %bitcast.77) | data formatting | bytes 1048576 | tf_op jit(solution)/shard_map/reshape;squeeze | solution.py:57
  9.2 6.3 %all-to-all-start.1 = ((bf16[4,128,512]{2,1,0:T(8,128)(2,1)}), bf16[4,128,512]{2,1,0:T(8,128)(2,1)S(1)}, u32[]{:S(2)}, u32[]{:S(2)}) async-start(bf16[4,128,512]{2,1,0:T(8,128)(2,1)} %bitcast.69), calls=%async_computation.1 | async-start | bytes 1048576 | tf_op jit(solution)/shard_map/all_to_all | solution.py:58
  15.5 1.2 copy.70
  16.7 1.1 copy.68
  17.9 17.8 %all-gather.2 = bf16[1,32,1024]{2,1,0:T(8,128)(2,1)S(1)} all-gather(bf16[1,8,1024]{2,1,0:T(8,128)(2,1)} %param.19), channel_id=4, replica_groups=mesh['clips'=2,'seq'=4,'tp'=2,'dp'=2] {'seq'}, dimensions={1}, use_global_device_ids=true | all-gather | bytes 81920 | tf_op jit(solution)/shard_map/all_gather | solution.py:149
  35.7 0.1 reshape.82
  35.8 0.3 fusion.57
  36.1 11.0 %pmax.7 = f32[32,16]{0,1:T(8,128)S(1)} all-reduce(f32[32,16]{0,1:T(8,128)S(1)} %get-tuple-element.56), channel_id=1, replica_groups=mesh['clips'=2,'seq'=4,'tp'=2,'dp'=2] {'seq'}, use_global_device_ids=true, to_apply=%region_5.6 | all-reduce | flops 512 | bytes 4096 | tf_op jit(solution)/shard_map/pmax | solution.py:91
  47.2 0.3 convolution_bitcast_fusion.1
  47.5 0.2 copy.71
  47.6 0.8 reshape.83
  48.5 0.4 reshape_squeeze.15
  48.9 0.9 copy.102
  49.7 0.4 reshape_squeeze.17
  50.1 0.9 copy.101
  51.0 0.2 copy.65
  51.2 13.2 %all-gather = bf16[1,32,1024]{2,1,0:T(8,128)(2,1)S(1)} all-gather(bf16[1,8,1024]{2,1,0:T(8,128)(2,1)S(1)} %copy-done.6), channel_id=2, replica_groups=mesh['clips'=2,'seq'=4,'tp'=2,'dp'=2] {'seq'}, dimensions={1}, use_global_device_ids=true | all-gather | bytes 81920 | tf_op jit(solution)/shard_map/all_gather | solution.py:150
  64.4 0.1 reshape.79
  64.5 0.3 fusion.34
  64.9 0.6 dynamic-slice
  66.1 15.7 %all-reduce = f32[32,16]{1,0:T(8,128)S(1)} all-reduce(f32[32,16]{1,0:T(8,128)S(1)} %copy.72), channel_id=6, replica_groups=mesh['clips'=2,'seq'=4,'tp'=2,'dp'=2] {'seq'}, use_global_device_ids=true, to_apply=%region_8.9.clone | all-reduce | flops 512 | bytes 4096
  82.0 0.2 fusion.56
  82.3 3.5 %all-to-all-start = ((bf16[4,128,512]{2,1,0:T(8,128)(2,1)}), bf16[4,128,512]{2,1,0:T(8,128)(2,1)S(1)}, u32[]{:S(2)}, u32[]{:S(2)}) async-start(bf16[4,128,512]{2,1,0:T(8,128)(2,1)} %bitcast.71), calls=%async_computation | async-start | bytes 1048576 | tf_op jit(solution)/shard_map/all_to_all | solution.py:65
  85.8 0.8 divide_convert_fusion
  86.6 4.4 %all_gather.18 = bf16[8,2048]{1,0:T(8,128)(2,1)S(1)} all-gather(bf16[8,1024]{1,0:T(8,128)(2,1)S(1)} %divide_convert_fusion), channel_id=1, replica_groups=mesh['clips'=2,'seq'=4,'tp'=2,'dp'=2] {'tp'}, dimensions={1}, use_global_device_ids=true | all-gather | bytes 49152 | tf_op jit(solution)/shard_map/all_gather | solution.py:109
  91.0 0.1 multiply_reduce_fusion
  91.2 13.9 %all_gather.19 = bf16[32,1024]{1,0:T(8,128)(2,1)S(1)} all-gather(bf16[8,1024]{1,0:T(8,128)(2,1)S(1)} %fusion.50), channel_id=1, replica_groups=mesh['clips'=2,'seq'=4,'tp'=2,'dp'=2] {'seq'}, dimensions={0}, use_global_device_ids=true | all-gather | bytes 81920 | tf_op jit(solution)/shard_map/all_gather | solution.py:118
  105.1 4.6 %all-to-all-start.2 = ((bf16[4,128,512]{2,1,0:T(8,128)(2,1)}), bf16[4,128,512]{2,1,0:T(8,128)(2,1)S(1)}, u32[]{:S(2)}, u32[]{:S(2)}) async-start(bf16[4,128,512]{2,1,0:T(8,128)(2,1)} %bitcast.70), calls=%async_computation.2 | async-start | bytes 1048576 | tf_op jit(solution)/shard_map/all_to_all | solution.py:66
  109.7 3.7 %fusion.58 = f32[32,2048]{1,0:T(8,128)} fusion(bf16[32,1024]{1,0:T(8,128)(2,1)S(1)} %all_gather.19, bf16[1024,2048]{1,0:T(8,128)(2,1)} %param.24), kind=kOutput, calls=%fused_computation.67 | convolution fusion | flops 134217728 | bytes 4521984 | tf_op jit(solution)/shard_map/dot_general | solution.py:117
  113.5 0.1 reshape.77
  113.7 0.7 bitcast_reduce_fusion
  114.5 1.9 %copy-done = f32[4,512,512]{2,1,0:T(8,128)} copy-done((f32[4,512,512]{2,1,0:T(8,128)}, f32[4,512,512]{2,1,0:T(8,128)S(1)}, u32[]{:S(2)}) %copy-start) | copy-done | bytes 4194328
  116.4 0.7 fusion.1
  117.1 7.5 %all-to-all-done.2 = bf16[4,128,512]{2,1,0:T(8,128)(2,1)S(1)} async-done(((bf16[4,128,512]{2,1,0:T(8,128)(2,1)}), bf16[4,128,512]{2,1,0:T(8,128)(2,1)S(1)}, u32[]{:S(2)}, u32[]{:S(2)}) %all-to-all-start.2) | async-done | bytes 524320 | tf_op jit(solution)/shard_map/all_to_all | solution.py:66
  124.8 3.4 %fusion.17 = bf16[512,4,128]{2,0,1:T(8,128)(2,1)S(1)} fusion(f32[4,512,512]{2,1,0:T(8,128)} %copy-done, f32[512,4]{0,1:T(4,128)S(1)} %get-tuple-element.52, bf16[512,4,128]{2,1,0:T(4,128)(2,1)S(1)} %reshape_reshape.11, f32[512,4]{0,1:T(4,128)S(1)} %fusion.1), kind=kOutput, calls=%fused_computation.18 | convolution fusion | flops 272105472 | bytes 5259264 | tf_op jit(solution)/shard_map/while/body/eval_jaxpr/qhk,khd->qhd/dot_general | solution.py:22
  128.2 0.4 copy.63
  128.6 1.0 convert_element_type.56
  129.6 3.5 %all-to-all-start.3 = ((bf16[4,128,512]{2,1,0:T(8,128)(2,1)}), bf16[4,128,512]{2,1,0:T(8,128)(2,1)S(1)}, u32[]{:S(2)}, u32[]{:S(2)}) async-start(bf16[4,128,512]{2,1,0:T(8,128)(2,1)} %convert_element_type.56), calls=%async_computation.3 | async-start | bytes 1048576 | tf_op jit(solution)/shard_map/all_to_all | solution.py:71
  133.1 5.3 %all-reduce.3.cloned.1.call-done = f32[32,2048]{1,0:T(8,128)} async-done(((f32[32,2048]{1,0:T(8,128)}), f32[32,2048]{1,0:T(8,128)}) %all-reduce.3.cloned.1.call-update) | async-done | bytes 262160 | tf_op jit(solution)/shard_map/psum | solution.py:122
  138.4 3.7 %fusion.38 = f32[32,1024]{1,0:T(8,128)} fusion(bf16[2048,1024]{1,0:T(8,128)(2,1)} %param.25, f32[32,2048]{1,0:T(8,128)} %all-reduce.3.cloned.1.call-done), kind=kOutput, calls=%fused_computation.41 | convolution fusion | flops 134807552 | bytes 4587520 | tf_op jit(solution)/shard_map/dot_general | solution.py:124
  142.1 13.3 %all-gather.1 = bf16[1,32,1024]{2,1,0:T(8,128)(2,1)S(1)} all-gather(bf16[1,8,1024]{2,1,0:T(8,128)(2,1)S(1)} %copy-done.7), channel_id=3, replica_groups=mesh['clips'=2,'seq'=4,'tp'=2,'dp'=2] {'seq'}, dimensions={1}, use_global_device_ids=true | all-gather | bytes 81920 | tf_op jit(solution)/shard_map/all_gather | solution.py:151
  155.4 0.1 reshape.81
  155.6 0.3 fusion.11
  155.8 0.9 copy.74
  156.7 5.1 %reduce-scatter.5.cloned.1.call-done = f32[8,1024]{1,0:T(8,128)} async-done(((f32[32,1024]{1,0:T(8,128)}), f32[8,1024]{1,0:T(8,128)}) %reduce-scatter.5.cloned.1.call-update) | async-done | bytes 32784 | tf_op jit(solution)/shard_map/reduce_scatter | solution.py:123
  161.8 1.4 convert_bitcast_fusion
  163.2 0.3 copy.64
  163.5 1.0 copy.73
  (39 shorter events, 0.9 us)
Async XLA Ops:
  7.2 41.3 %copy-start.1 = (bf16[1,128,2048]{2,1,0:T(8,128)(2,1)S(1)}, bf16[1,128,2048]{2,1,0:T(8,128)(2,1)}, u32[]{:S(2)}) copy-start(bf16[1,128,2048]{2,1,0:T(8,128)(2,1)} %param.14) | copy-start | bytes 1572868
  7.2 42.6 %copy-start.2 = (bf16[1,128,2048]{2,1,0:T(8,128)(2,1)S(1)}, bf16[1,128,2048]{2,1,0:T(8,128)(2,1)}, u32[]{:S(2)}) copy-start(bf16[1,128,2048]{2,1,0:T(8,128)(2,1)} %param.15) | copy-start | bytes 1572868
  9.2 73.1 %all-to-all-start.1 = ((bf16[4,128,512]{2,1,0:T(8,128)(2,1)}), bf16[4,128,512]{2,1,0:T(8,128)(2,1)S(1)}, u32[]{:S(2)}, u32[]{:S(2)}) async-start(bf16[4,128,512]{2,1,0:T(8,128)(2,1)} %bitcast.69), calls=%async_computation.1 | async-start | bytes 1048576 | tf_op jit(solution)/shard_map/all_to_all | solution.py:58
  15.5 35.5 %copy-start.3 = (bf16[1,128,1024]{2,1,0:T(8,128)(2,1)S(1)}, bf16[1,128,1024]{2,1,0:T(8,128)(2,1)}, u32[]{:S(2)}) copy-start(bf16[1,128,1024]{2,1,0:T(8,128)(2,1)} %param.16) | copy-start | bytes 786436
  15.5 35.7 %copy-start.6 = (bf16[1,8,1024]{2,1,0:T(8,128)(2,1)S(1)}, bf16[1,8,1024]{2,1,0:T(8,128)(2,1)}, u32[]{:S(2)}) copy-start(bf16[1,8,1024]{2,1,0:T(8,128)(2,1)} %param.17) | copy-start | bytes 49156
  15.5 70.3 %reduce-scatter.3.cloned.1.call-start = ((), (), s32[]{:S(2)}) async-start(), calls=%async_computation.6 | async-start | bytes 163840 | tf_op jit(solution)/shard_map/reduce_scatter | solution.py:103
  17.8 47.0 %copy-start.9 = (u32[32]{0:T(128)S(1)}, u32[32]{0:T(128)}, u32[]{:S(2)}) copy-start(u32[32]{0:T(128)} %constant.75) | copy-start | bytes 388
  17.8 64.2 %copy-start.8 = (f32[2048]{0:T(1024)S(1)}, f32[2048]{0:T(1024)}, u32[]{:S(2)}) copy-start(f32[2048]{0:T(1024)} %param.23) | copy-start | bytes 24580
  47.6 43.4 %copy-start.5 = (bf16[1,8,2048]{2,1,0:T(8,128)(2,1)S(1)}, bf16[1,8,2048]{2,1,0:T(8,128)(2,1)}, u32[]{:S(2)}) copy-start(bf16[1,8,2048]{2,1,0:T(8,128)(2,1)} %param.22) | copy-start | bytes 98308
  82.3 22.8 %all-to-all-start = ((bf16[4,128,512]{2,1,0:T(8,128)(2,1)}), bf16[4,128,512]{2,1,0:T(8,128)(2,1)S(1)}, u32[]{:S(2)}, u32[]{:S(2)}) async-start(bf16[4,128,512]{2,1,0:T(8,128)(2,1)} %bitcast.71), calls=%async_computation | async-start | bytes 1048576 | tf_op jit(solution)/shard_map/all_to_all | solution.py:65
  86.6 27.9 %copy-start.4 = (bf16[8,1024]{1,0:T(8,128)(2,1)}, bf16[8,1024]{1,0:T(8,128)(2,1)S(1)}, u32[]{:S(2)}) copy-start(bf16[8,1024]{1,0:T(8,128)(2,1)S(1)} %divide_convert_fusion) | copy-start | bytes 49156
  105.1 19.5 %all-to-all-start.2 = ((bf16[4,128,512]{2,1,0:T(8,128)(2,1)}), bf16[4,128,512]{2,1,0:T(8,128)(2,1)S(1)}, u32[]{:S(2)}, u32[]{:S(2)}) async-start(bf16[4,128,512]{2,1,0:T(8,128)(2,1)} %bitcast.70), calls=%async_computation.2 | async-start | bytes 1048576 | tf_op jit(solution)/shard_map/all_to_all | solution.py:66
  109.7 28.7 %all-reduce.3.cloned.1.call-start = ((), (), s32[]{:S(2)}) async-start(), calls=%async_computation.7 | async-start | bytes 524288 | tf_op jit(solution)/shard_map/psum | solution.py:122
  114.5 1.9 %copy-start = (f32[4,512,512]{2,1,0:T(8,128)}, f32[4,512,512]{2,1,0:T(8,128)S(1)}, u32[]{:S(2)}) copy-start(f32[4,512,512]{2,1,0:T(8,128)S(1)} %get-tuple-element.53) | copy-start | bytes 12582916
  128.1 14.0 %copy-start.7 = (bf16[1,8,1024]{2,1,0:T(8,128)(2,1)S(1)}, bf16[1,8,1024]{2,1,0:T(8,128)(2,1)}, u32[]{:S(2)}) copy-start(bf16[1,8,1024]{2,1,0:T(8,128)(2,1)} %param.18) | copy-start | bytes 49156
  129.6 33.6 %all-to-all-start.3 = ((bf16[4,128,512]{2,1,0:T(8,128)(2,1)}), bf16[4,128,512]{2,1,0:T(8,128)(2,1)S(1)}, u32[]{:S(2)}, u32[]{:S(2)}) async-start(bf16[4,128,512]{2,1,0:T(8,128)(2,1)} %convert_element_type.56), calls=%async_computation.3 | async-start | bytes 1048576 | tf_op jit(solution)/shard_map/all_to_all | solution.py:71
  133.0 28.8 %reduce-scatter.5.cloned.1.call-start = ((), (), s32[]{:S(2)}) async-start(), calls=%async_computation.8 | async-start | bytes 163840 | tf_op jit(solution)/shard_map/reduce_scatter | solution.py:123
Sparse Core Ops, SparseCore 0:
  48.6 17.6 reduce-scatter.2
  113.6 24.7 all-reduce.2
  142.2 19.5 reduce-scatter.4
where the time goes:
time: 172 us; the launch traced here: 171 us
  blocking collectives  89.4 us (52%)
  starting transfers between devices  18 us (10%)
  waiting for transfers between devices  18 us (10%)
  local copies, waits for them, and re-layouts  15 us (9%)
  between operations  14.7 us (9%)
  matrix products  12.6 us (7%)
  other arithmetic  3.38 us (2%)
    all_gather x1, blocking collectives, body(): gathered_query = lax.all_gather(audio_query[0], 'seq', axis=0, tiled=True)  17.8 us
    unnamed x1, blocking collectives  15.7 us
    all_gather x1, blocking collectives, audio_block(): lax.all_gather(own_features, 'seq', axis=0, tiled=True)  13.9 us
    all_gather x1, blocking collectives, body(): gathered_value = lax.all_gather(audio_value[0], 'seq', axis=0, tiled=True)  13.3 us
    all_gather x1, blocking collectives, body(): gathered_key = lax.all_gather(audio_key[0], 'seq', axis=0, tiled=True)  13.2 us
    pmax x1, blocking collectives, audio_listen(): peak_value = lax.pmax(local_peak, 'seq')  11 us
    all_to_all x1, waiting for transfers between devices, video_self(): lax.all_to_all(spread(values_in), 'seq', split_axis=0, concat_axis=0, til...  7.52 us
    unnamed x27, local copies, waits for them, and re-layouts  6.86 us
  transfers between devices with their start and end apart: 7, of which 3 were waited for; matrix products, arithmetic and copies ran while one was open for 15% of the time, Pallas kernels for 0%

commit v1 on v0

--- a/solution.py
+++ b/solution.py
@@ -3,6 +3,7 @@
 import jax.numpy as jnp
 from jax import lax
 from jax.sharding import PartitionSpec as P
+from jax.lax import axis_index, ppermute, psum
 
 VHEAD = 128
 CHEAD = 64
@@ -147,7 +148,30 @@
     cross_heads = cross_query.shape[2] // CHEAD
     mixed_list.append(video_self(video_query[0], video_key[0], video_value[0]))
     gathered_query = lax.all_gather(audio_query[0], "seq", axis=0, tiled=True)
-    gathered_key = lax.all_gather(audio_key[0], "seq", axis=0, tiled=True)
+
+    def compute_floor(mine_x):
+        latest = psum(1, "seq")
+        later = axis_index("seq")
+        prior, tmp, block_now = (latest, later, mine_x.shape[0])
+        pages = [(to_i, (to_i + 1) % prior) for to_i in range(prior)]
+        stack_in = [(to_i, (to_i - 1) % prior) for to_i in range(prior)]
+        near = jnp.zeros((*mine_x.shape[:0], prior * block_now, *mine_x.shape[1:]), mine_x.dtype)
+        near = lax.dynamic_update_slice_in_dim(near, mine_x, tmp * block_now, axis=0)
+        kept_arr = prior // 2
+        block_last = outcome_arr = mine_x
+        for d in tuple(range(1, kept_arr + 1)):
+            block_last = ppermute(block_last, axis_name="seq", perm=pages)
+            near = lax.dynamic_update_slice_in_dim(
+                near, block_last, (tmp - d) % prior * block_now, axis=0
+            )
+            if d < prior - kept_arr:
+                outcome_arr = ppermute(outcome_arr, "seq", stack_in)
+                near = lax.dynamic_update_slice_in_dim(
+                    near, outcome_arr, (tmp + d) % prior * block_now, axis=0
+                )
+        return near
+
+    gathered_key = compute_floor(audio_key[0])
     gathered_value = lax.all_gather(audio_value[0], "seq", axis=0, tiled=True)
     heard_list.append(attend(cross_query[0], gathered_key, gathered_value, cross_heads))
     audio_seen = audio_listen(gathered_query, cross_key[0], cross_value[0], cross_heads)

time: 172 us -> 180 us (1.047)
  waiting for transfers between devices: 18 us -> 37.1 us
  blocking collectives: 89.4 us -> 76.4 us
    reduce_scatter x1, waiting for transfers between devices: 5.12 us -> 18.4 us  [audio_block(): lax.psum_scatter(jnp.dot(hidden, down_weight, preferred_element_type=jnp....]
    all_gather x1 -> x0, blocking collectives: 13.2 us -> none  [body(): gathered_key = lax.all_gather(audio_key[0], 'seq', axis=0, tiled=True)]
    ppermute x0 -> x3, waiting for transfers between devices: none -> 5.76 us  [the longest x2 5.76 us: compute_floor(): block_last = ppermute(block_last, axis_name='seq', perm=pages)]
    ppermute x0 -> x3, starting transfers between devices: none -> 5.26 us  [the longest x2 3.16 us: compute_floor(): block_last = ppermute(block_last, axis_name='seq', perm=pages)]
    all_to_all x1, starting transfers between devices: 6.35 us -> 3.47 us  [video_self(): lax.all_to_all(shaped.reshape(seq_count, block_tokens, group_width), 'seq...]
  transfers between devices with their start and end apart: 7 -> 10, of which waited for: 3 -> 4; matrix products, arithmetic and copies ran while one was open for 15% -> 16% of each run, Pallas kernels for 0% -> 0%
where the time goes in v1:
time: 180 us; the launch traced here: 179 us
  blocking collectives  76.4 us (42%)
  waiting for transfers between devices  37.1 us (21%)
  starting transfers between devices  19.6 us (11%)
  local copies, waits for them, and re-layouts  15 us (8%)
  between operations  14.8 us (8%)
  matrix products  12.6 us (7%)
  other arithmetic  3.38 us (2%)
    reduce_scatter x1, waiting for transfers between devices, audio_block(): lax.psum_scatter(jnp.dot(hidden, down_weight, preferred_element_type=jnp....  18.4 us
    all_gather x1, blocking collectives, body(): gathered_query = lax.all_gather(audio_query[0], 'seq', axis=0, tiled=True)  17.8 us
    unnamed x1, blocking collectives  15.6 us
    all_gather x1, blocking collectives, audio_block(): lax.all_gather(own_features, 'seq', axis=0, tiled=True)  14.6 us
    all_gather x1, blocking collectives, body(): gathered_value = lax.all_gather(audio_value[0], 'seq', axis=0, tiled=True)  13.1 us
    pmax x1, blocking collectives, audio_listen(): peak_value = lax.pmax(local_peak, 'seq')  10.9 us
    all_to_all x1, waiting for transfers between devices, video_self(): lax.all_to_all(spread(values_in), 'seq', split_axis=0, concat_axis=0, til...  8.28 us
    unnamed x27, local copies, waits for them, and re-layouts  6.88 us
  transfers between devices with their start and end apart: 10, of which 4 were waited for; matrix products, arithmetic and copies ran while one was open for 16% of the time, Pallas kernels for 0%

profile of v1, /device:TPU:0, one launch (start us, length us, event | category | flops | bytes accessed | tf_op | source)
XLA Modules:
  0.0 178.9 jit_solution(8982733720187454643)
XLA Ops:
  7.2 3.1 %collective-permute-start = (bf16[8,1024]{1,0:T(8,128)(2,1)}, bf16[8,1024]{1,0:T(8,128)(2,1)S(1)}, u32[]{:S(2)}, u32[]{:S(2)}) collective-permute-start(bf16[8,1024]{1,0:T(8,128)(2,1)} %bitcast.82), channel_id=1, source_target_pairs={{0,4},{4,8},{8,12},{12,0},{1,5},{5,9},{9,13},{13,1},{2,6},{6,10},{... | collective-permute-start | bytes 49160 | tf_op jit(solution)/shard_map/ppermute | solution.py:163
  10.3 2.1 %collective-permute-start.1 = (bf16[8,1024]{1,0:T(8,128)(2,1)}, bf16[8,1024]{1,0:T(8,128)(2,1)S(1)}, u32[]{:S(2)}, u32[]{:S(2)}) collective-permute-start(bf16[8,1024]{1,0:T(8,128)(2,1)} %bitcast.83), channel_id=1, source_target_pairs={{0,12},{4,0},{8,4},{12,8},{1,13},{5,1},{9,5},{13,9},{2,14},{6,2},{... | collective-permute-start | bytes 49160 | tf_op jit(solution)/shard_map/ppermute | solution.py:168
  12.4 1.9 %copy.100 = bf16[1,16,4,8,512]{4,3,1,2,0:T(8,128)(2,1)} copy(bf16[1,16,4,8,512]{4,3,2,1,0:T(8,128)(2,1)} %bitcast.79) | data formatting | bytes 1048576 | tf_op jit(solution)/shard_map/reshape;squeeze | solution.py:58
  14.3 3.5 %all-to-all-start.1 = ((bf16[4,128,512]{2,1,0:T(8,128)(2,1)}), bf16[4,128,512]{2,1,0:T(8,128)(2,1)S(1)}, u32[]{:S(2)}, u32[]{:S(2)}) async-start(bf16[4,128,512]{2,1,0:T(8,128)(2,1)} %bitcast.71), calls=%async_computation.1 | async-start | bytes 1048576 | tf_op jit(solution)/shard_map/all_to_all | solution.py:59
  17.9 1.2 copy.70
  19.1 1.1 copy.68
  20.2 17.8 %all-gather.1 = bf16[1,32,1024]{2,1,0:T(8,128)(2,1)S(1)} all-gather(bf16[1,8,1024]{2,1,0:T(8,128)(2,1)} %param.19), channel_id=3, replica_groups=mesh['clips'=2,'seq'=4,'tp'=2,'dp'=2] {'seq'}, dimensions={1}, use_global_device_ids=true | all-gather | bytes 81920 | tf_op jit(solution)/shard_map/all_gather | solution.py:150
  38.0 0.1 reshape.82
  38.2 0.3 fusion.57
  38.5 10.9 %pmax.7 = f32[32,16]{0,1:T(8,128)S(1)} all-reduce(f32[32,16]{0,1:T(8,128)S(1)} %get-tuple-element.56), channel_id=1, replica_groups=mesh['clips'=2,'seq'=4,'tp'=2,'dp'=2] {'seq'}, use_global_device_ids=true, to_apply=%region_5.6 | all-reduce | flops 512 | bytes 4096 | tf_op jit(solution)/shard_map/pmax | solution.py:92
  49.4 0.3 convolution_bitcast_fusion.1
  49.7 0.2 copy.71
  49.9 0.8 reshape.83
  50.8 0.3 fusion.34
  51.1 0.4 reshape_squeeze.15
  51.4 0.9 copy.102
  52.3 0.4 reshape_squeeze.17
  52.7 0.9 copy.101
  53.6 0.2 copy.65
  53.8 15.6 %all-reduce = f32[32,16]{1,0:T(8,128)S(1)} all-reduce(f32[32,16]{1,0:T(8,128)S(1)} %copy.72), channel_id=5, replica_groups=mesh['clips'=2,'seq'=4,'tp'=2,'dp'=2] {'seq'}, use_global_device_ids=true, to_apply=%region_8.9.clone | all-reduce | flops 512 | bytes 4096
  69.4 0.6 dynamic-slice
  70.7 13.1 %all-gather = bf16[1,32,1024]{2,1,0:T(8,128)(2,1)S(1)} all-gather(bf16[1,8,1024]{2,1,0:T(8,128)(2,1)S(1)} %copy-done.6), channel_id=2, replica_groups=mesh['clips'=2,'seq'=4,'tp'=2,'dp'=2] {'seq'}, dimensions={1}, use_global_device_ids=true | all-gather | bytes 81920 | tf_op jit(solution)/shard_map/all_gather | solution.py:175
  83.8 0.1 reshape.81
  84.3 5.8 %collective-permute-done.2 = bf16[8,1024]{1,0:T(8,128)(2,1)S(1)} collective-permute-done((bf16[8,1024]{1,0:T(8,128)(2,1)S(1)}, bf16[8,1024]{1,0:T(8,128)(2,1)S(1)}, u32[]{:S(2)}, u32[]{:S(2)}) %collective-permute-start.2) | collective-permute-done | bytes 16416 | tf_op jit(solution)/shard_map/ppermute | solution.py:163
  90.1 0.1 reshape.79
  90.2 0.2 fusion.56
  90.4 3.5 %all-to-all-start = ((bf16[4,128,512]{2,1,0:T(8,128)(2,1)}), bf16[4,128,512]{2,1,0:T(8,128)(2,1)S(1)}, u32[]{:S(2)}, u32[]{:S(2)}) async-start(bf16[4,128,512]{2,1,0:T(8,128)(2,1)} %bitcast.73), calls=%async_computation | async-start | bytes 1048576 | tf_op jit(solution)/shard_map/all_to_all | solution.py:66
  93.9 0.8 divide_convert_fusion
  94.7 4.4 %all_gather.14 = bf16[8,2048]{1,0:T(8,128)(2,1)S(1)} all-gather(bf16[8,1024]{1,0:T(8,128)(2,1)S(1)} %divide_convert_fusion), channel_id=1, replica_groups=mesh['clips'=2,'seq'=4,'tp'=2,'dp'=2] {'tp'}, dimensions={1}, use_global_device_ids=true | all-gather | bytes 49152 | tf_op jit(solution)/shard_map/all_gather | solution.py:110
  99.4 14.6 %all_gather.15 = bf16[32,1024]{1,0:T(8,128)(2,1)S(1)} all-gather(bf16[8,1024]{1,0:T(8,128)(2,1)S(1)} %fusion.50), channel_id=1, replica_groups=mesh['clips'=2,'seq'=4,'tp'=2,'dp'=2] {'seq'}, dimensions={0}, use_global_device_ids=true | all-gather | bytes 81920 | tf_op jit(solution)/shard_map/all_gather | solution.py:119
  113.9 3.8 %all-to-all-start.2 = ((bf16[4,128,512]{2,1,0:T(8,128)(2,1)}), bf16[4,128,512]{2,1,0:T(8,128)(2,1)S(1)}, u32[]{:S(2)}, u32[]{:S(2)}) async-start(bf16[4,128,512]{2,1,0:T(8,128)(2,1)} %bitcast.72), calls=%async_computation.2 | async-start | bytes 1048576 | tf_op jit(solution)/shard_map/all_to_all | solution.py:67
  117.7 3.7 %fusion.58 = f32[32,2048]{1,0:T(8,128)} fusion(bf16[32,1024]{1,0:T(8,128)(2,1)S(1)} %all_gather.15, bf16[1024,2048]{1,0:T(8,128)(2,1)} %param.24), kind=kOutput, calls=%fused_computation.71 | convolution fusion | flops 134217728 | bytes 4521984 | tf_op jit(solution)/shard_map/dot_general | solution.py:118
  121.7 0.7 bitcast_reduce_fusion
  122.5 1.9 %copy-done = f32[4,512,512]{2,1,0:T(8,128)} copy-done((f32[4,512,512]{2,1,0:T(8,128)}, f32[4,512,512]{2,1,0:T(8,128)S(1)}, u32[]{:S(2)}) %copy-start) | copy-done | bytes 4194328
  124.4 0.7 fusion.1
  125.1 8.3 %all-to-all-done.2 = bf16[4,128,512]{2,1,0:T(8,128)(2,1)S(1)} async-done(((bf16[4,128,512]{2,1,0:T(8,128)(2,1)}), bf16[4,128,512]{2,1,0:T(8,128)(2,1)S(1)}, u32[]{:S(2)}, u32[]{:S(2)}) %all-to-all-start.2) | async-done | bytes 524320 | tf_op jit(solution)/shard_map/all_to_all | solution.py:67
  133.5 3.4 %fusion.17 = bf16[512,4,128]{2,0,1:T(8,128)(2,1)S(1)} fusion(f32[4,512,512]{2,1,0:T(8,128)} %copy-done, f32[512,4]{0,1:T(4,128)S(1)} %get-tuple-element.52, bf16[512,4,128]{2,1,0:T(4,128)(2,1)S(1)} %reshape_reshape.11, f32[512,4]{0,1:T(4,128)S(1)} %fusion.1), kind=kOutput, calls=%fused_computation.18 | convolution fusion | flops 272105472 | bytes 5259264 | tf_op jit(solution)/shard_map/while/body/eval_jaxpr/qhk,khd->qhd/dot_general | solution.py:23
  136.9 0.4 copy.63
  137.3 1.0 convert_element_type.56
  138.3 3.5 %all-to-all-start.3 = ((bf16[4,128,512]{2,1,0:T(8,128)(2,1)}), bf16[4,128,512]{2,1,0:T(8,128)(2,1)S(1)}, u32[]{:S(2)}, u32[]{:S(2)}) async-start(bf16[4,128,512]{2,1,0:T(8,128)(2,1)} %convert_element_type.56), calls=%async_computation.3 | async-start | bytes 1048576 | tf_op jit(solution)/shard_map/all_to_all | solution.py:72
  141.8 4.6 %all-reduce.3.cloned.1.call-done = f32[32,2048]{1,0:T(8,128)} async-done(((f32[32,2048]{1,0:T(8,128)}), f32[32,2048]{1,0:T(8,128)}) %all-reduce.3.cloned.1.call-update) | async-done | bytes 262160 | tf_op jit(solution)/shard_map/psum | solution.py:123
  146.4 3.7 %fusion.38 = f32[32,1024]{1,0:T(8,128)} fusion(bf16[2048,1024]{1,0:T(8,128)(2,1)} %param.25, f32[32,2048]{1,0:T(8,128)} %all-reduce.3.cloned.1.call-done), kind=kOutput, calls=%fused_computation.41 | convolution fusion | flops 134807552 | bytes 4587520 | tf_op jit(solution)/shard_map/dot_general | solution.py:125
  150.2 0.3 fusion.11
  150.5 0.9 copy.74
  151.3 18.4 %reduce-scatter.5.cloned.1.call-done = f32[8,1024]{1,0:T(8,128)} async-done(((f32[32,1024]{1,0:T(8,128)}), f32[8,1024]{1,0:T(8,128)}) %reduce-scatter.5.cloned.1.call-update) | async-done | bytes 32784 | tf_op jit(solution)/shard_map/reduce_scatter | solution.py:124
  169.7 1.4 convert_bitcast_fusion
  171.1 0.3 copy.64
  171.4 1.0 copy.73
  (49 shorter events, 1.2 us)
Async XLA Ops:
  7.2 43.9 %copy-start.1 = (bf16[1,128,2048]{2,1,0:T(8,128)(2,1)S(1)}, bf16[1,128,2048]{2,1,0:T(8,128)(2,1)}, u32[]{:S(2)}) copy-start(bf16[1,128,2048]{2,1,0:T(8,128)(2,1)} %param.14) | copy-start | bytes 1572868
  7.2 77.0 %collective-permute-start = (bf16[8,1024]{1,0:T(8,128)(2,1)}, bf16[8,1024]{1,0:T(8,128)(2,1)S(1)}, u32[]{:S(2)}, u32[]{:S(2)}) collective-permute-start(bf16[8,1024]{1,0:T(8,128)(2,1)} %bitcast.82), channel_id=1, source_target_pairs={{0,4},{4,8},{8,12},{12,0},{1,5},{5,9},{9,13},{13,1},{2,6},{6,10},{... | collective-permute-start | bytes 49160 | tf_op jit(solution)/shard_map/ppermute | solution.py:163
  10.3 74.0 %collective-permute-start.1 = (bf16[8,1024]{1,0:T(8,128)(2,1)}, bf16[8,1024]{1,0:T(8,128)(2,1)S(1)}, u32[]{:S(2)}, u32[]{:S(2)}) collective-permute-start(bf16[8,1024]{1,0:T(8,128)(2,1)} %bitcast.83), channel_id=1, source_target_pairs={{0,12},{4,0},{8,4},{12,8},{1,13},{5,1},{9,5},{13,9},{2,14},{6,2},{... | collective-permute-start | bytes 49160 | tf_op jit(solution)/shard_map/ppermute | solution.py:168
  12.4 39.9 %copy-start.2 = (bf16[1,128,2048]{2,1,0:T(8,128)(2,1)S(1)}, bf16[1,128,2048]{2,1,0:T(8,128)(2,1)}, u32[]{:S(2)}) copy-start(bf16[1,128,2048]{2,1,0:T(8,128)(2,1)} %param.15) | copy-start | bytes 1572868
  14.3 76.1 %all-to-all-start.1 = ((bf16[4,128,512]{2,1,0:T(8,128)(2,1)}), bf16[4,128,512]{2,1,0:T(8,128)(2,1)S(1)}, u32[]{:S(2)}, u32[]{:S(2)}) async-start(bf16[4,128,512]{2,1,0:T(8,128)(2,1)} %bitcast.71), calls=%async_computation.1 | async-start | bytes 1048576 | tf_op jit(solution)/shard_map/all_to_all | solution.py:59
  17.8 35.8 %copy-start.3 = (bf16[1,128,1024]{2,1,0:T(8,128)(2,1)S(1)}, bf16[1,128,1024]{2,1,0:T(8,128)(2,1)}, u32[]{:S(2)}) copy-start(bf16[1,128,1024]{2,1,0:T(8,128)(2,1)} %param.16) | copy-start | bytes 786436
  17.8 76.1 %reduce-scatter.3.cloned.1.call-start = ((), (), s32[]{:S(2)}) async-start(), calls=%async_computation.6 | async-start | bytes 163840 | tf_op jit(solution)/shard_map/reduce_scatter | solution.py:104
  19.0 50.4 %copy-start.9 = (u32[32]{0:T(128)S(1)}, u32[32]{0:T(128)}, u32[]{:S(2)}) copy-start(u32[32]{0:T(128)} %constant.113) | copy-start | bytes 388
  19.0 51.7 %copy-start.7 = (bf16[1,8,1024]{2,1,0:T(8,128)(2,1)S(1)}, bf16[1,8,1024]{2,1,0:T(8,128)(2,1)}, u32[]{:S(2)}) copy-start(bf16[1,8,1024]{2,1,0:T(8,128)(2,1)} %param.17) | copy-start | bytes 49156
  19.0 51.7 %copy-start.6 = (bf16[1,8,1024]{2,1,0:T(8,128)(2,1)S(1)}, bf16[1,8,1024]{2,1,0:T(8,128)(2,1)}, u32[]{:S(2)}) copy-start(bf16[1,8,1024]{2,1,0:T(8,128)(2,1)} %param.18) | copy-start | bytes 49156
  38.2 46.0 %copy-start.8 = (f32[2048]{0:T(1024)S(1)}, f32[2048]{0:T(1024)}, u32[]{:S(2)}) copy-start(f32[2048]{0:T(1024)} %param.23) | copy-start | bytes 24580
  49.9 49.2 %copy-start.5 = (bf16[1,8,2048]{2,1,0:T(8,128)(2,1)S(1)}, bf16[1,8,2048]{2,1,0:T(8,128)(2,1)}, u32[]{:S(2)}) copy-start(bf16[1,8,2048]{2,1,0:T(8,128)(2,1)} %param.22) | copy-start | bytes 98308
  84.2 5.9 %collective-permute-start.2 = (bf16[8,1024]{1,0:T(8,128)(2,1)S(1)}, bf16[8,1024]{1,0:T(8,128)(2,1)S(1)}, u32[]{:S(2)}, u32[]{:S(2)}) collective-permute-start(bf16[8,1024]{1,0:T(8,128)(2,1)S(1)} %collective-permute-done), channel_id=1, source_target_pairs={{0,4},{4,8},{8,12},{12,0},{1,5},{5,9},{9,13},{13,1},{2,6},{6,10},{... | collective-permute-start | bytes 49160 | tf_op jit(solution)/shard_map/ppermute | solution.py:163
  90.4 23.5 %all-to-all-start = ((bf16[4,128,512]{2,1,0:T(8,128)(2,1)}), bf16[4,128,512]{2,1,0:T(8,128)(2,1)S(1)}, u32[]{:S(2)}, u32[]{:S(2)}) async-start(bf16[4,128,512]{2,1,0:T(8,128)(2,1)} %bitcast.73), calls=%async_computation | async-start | bytes 1048576 | tf_op jit(solution)/shard_map/all_to_all | solution.py:66
  94.7 27.7 %copy-start.4 = (bf16[8,1024]{1,0:T(8,128)(2,1)}, bf16[8,1024]{1,0:T(8,128)(2,1)S(1)}, u32[]{:S(2)}) copy-start(bf16[8,1024]{1,0:T(8,128)(2,1)S(1)} %divide_convert_fusion) | copy-start | bytes 49156
  113.9 19.4 %all-to-all-start.2 = ((bf16[4,128,512]{2,1,0:T(8,128)(2,1)}), bf16[4,128,512]{2,1,0:T(8,128)(2,1)S(1)}, u32[]{:S(2)}, u32[]{:S(2)}) async-start(bf16[4,128,512]{2,1,0:T(8,128)(2,1)} %bitcast.72), calls=%async_computation.2 | async-start | bytes 1048576 | tf_op jit(solution)/shard_map/all_to_all | solution.py:67
  117.7 28.7 %all-reduce.3.cloned.1.call-start = ((), (), s32[]{:S(2)}) async-start(), calls=%async_computation.7 | async-start | bytes 524288 | tf_op jit(solution)/shard_map/psum | solution.py:123
  122.5 1.9 %copy-start = (f32[4,512,512]{2,1,0:T(8,128)}, f32[4,512,512]{2,1,0:T(8,128)S(1)}, u32[]{:S(2)}) copy-start(f32[4,512,512]{2,1,0:T(8,128)S(1)} %get-tuple-element.53) | copy-start | bytes 12582916
  138.3 32.8 %all-to-all-start.3 = ((bf16[4,128,512]{2,1,0:T(8,128)(2,1)}), bf16[4,128,512]{2,1,0:T(8,128)(2,1)S(1)}, u32[]{:S(2)}, u32[]{:S(2)}) async-start(bf16[4,128,512]{2,1,0:T(8,128)(2,1)} %convert_element_type.56), calls=%async_computation.3 | async-start | bytes 1048576 | tf_op jit(solution)/shard_map/all_to_all | solution.py:72
  141.8 28.0 %reduce-scatter.5.cloned.1.call-start = ((), (), s32[]{:S(2)}) async-start(), calls=%async_computation.8 | async-start | bytes 163840 | tf_op jit(solution)/shard_map/reduce_scatter | solution.py:124
Sparse Core Ops, SparseCore 0:
  50.8 17.6 reduce-scatter.2
  121.6 24.7 all-reduce.2
  150.2 19.4 reduce-scatter.4
